TPU v7x, 32 devices: a whole 2x2x4 slice. The times are simulated.
32 devices in a mesh: groups: 2 (over y), choice: 16 (over z, x, core).
Axes of the slice: x: 2, y: 2, z: 4, core: 2. Of those that a mesh axis runs over, the one named last changes fastest.
Arguments:
- transitions: bfloat16 [4096, 6, 128, 128], P('choice'), may hold values from -0.21875 to 0.21875
- col_block: int32 [4096, 6], P('choice'), may hold values from 0 to 63
- reward_class: int32 [4, 4096, 128], P(None, 'choice'), may hold values from 0 to 127
- reward_table: bfloat16 [4, 128, 256], P(None, None, 'groups'), parts along dimension 2, may hold values from -6 to 310
- terminal: bfloat16 [8192, 256], P('choice', 'groups'), parts along dimension 1, may hold values from -6 to 6
Outputs:
- values: float32 [8192, 256], P('choice', 'groups'), parts along dimension 1
There are 2 independent parts, one for each index of `groups`. A program takes and returns all parts, laid end to end along the dimension named above; an argument that names none is the same for every part. Nothing has to cross between parts.
All inputs are finite; a program needn't handle non-finite values.
Results may differ from a plain program's by a relative error of at most 0.0013.
Values may be sent and summed in bfloat16 or wider, within the bound.
A program may use at most 256 MiB of HBM per device.

v0:
```python
import jax
import jax.numpy as jnp
from jax import lax
from jax.sharding import PartitionSpec as P

J = 64
AGES = 4
STATES = 8192


def partner(array, axis, apart):
    return lax.ppermute(array, axis, [(i, i ^ 1 << apart) for i in range(lax.axis_size(axis))])


def combine(earlier, later):
    highest = jnp.maximum(earlier[0], later[0])
    totals = earlier[1] * jnp.exp(earlier[0] - highest) + later[1] * jnp.exp(later[0] - highest)
    return (highest, totals)


def choice_partials(transitions, col_block, classes, reward_rows, next_values):
    pair_count = transitions.shape[0]
    block_rows = transitions.shape[2]
    columns = next_values.shape[1]
    stacked = next_values.reshape(STATES // block_rows, block_rows, columns)
    picked = jnp.take(stacked, col_block, axis=0)
    expected = jnp.einsum("pkab,pkbq->paq", transitions, picked, preferred_element_type=jnp.float32)
    onehot = (classes[:, :, None] == jnp.arange(reward_rows.shape[0], dtype=jnp.int32)).astype(
        jnp.bfloat16
    )
    reward = jnp.einsum("pbr,rq->pbq", onehot, reward_rows, preferred_element_type=jnp.float32)
    scores = expected + reward
    inner_count = min(J, pair_count)
    grouped = scores.reshape(pair_count // inner_count, inner_count, block_rows, columns)
    highest = jnp.max(grouped, axis=1)
    totals = jnp.sum(jnp.exp(grouped - highest[:, None]), axis=1)
    return (highest.reshape(-1, columns), totals.reshape(-1, columns))


def shards(transitions, col_block, reward_class, reward_table, terminal):
    devices = lax.axis_size("choice")
    pair_count = transitions.shape[0]
    inner_count = min(J, pair_count)
    group_size = J // inner_count
    swap_count = group_size.bit_length() - 1
    member_index = lax.axis_index("choice") % group_size
    share_rows = STATES // devices
    next_values = lax.all_gather(terminal, "choice", axis=0, tiled=True)
    result = None
    for age_index in range(AGES - 1, -1, -1):
        highest, totals = choice_partials(
            transitions, col_block, reward_class[age_index], reward_table[age_index], next_values
        )
        for bit_index in range(swap_count):
            incoming = partner((highest, totals), "choice", bit_index)
            highest, totals = combine((highest, totals), incoming)
        block_values = highest + jnp.log(totals)
        if age_index > 0:
            gathered = lax.all_gather(
                block_values.astype(jnp.bfloat16), "choice", axis=0, tiled=True
            )
            spread = gathered.astype(jnp.float32).reshape(
                devices // group_size, group_size, block_values.shape[0], block_values.shape[1]
            )
            next_values = (
                jnp.mean(spread, axis=1).astype(jnp.bfloat16).reshape(STATES, block_values.shape[1])
            )
        else:
            result = lax.dynamic_slice_in_dim(
                block_values, member_index * share_rows, share_rows, 0
            )
    return result


def solution(mesh):
    return jax.shard_map(
        shards,
        mesh=mesh,
        in_specs=(
            P("choice", None, None, None),
            P("choice", None),
            P(None, "choice", None),
            P(None, None, "groups"),
            P("choice", "groups"),
        ),
        out_specs=P("choice", "groups"),
        check_vma=False,
    )
```

profile of v0, /device:TPU:0, one launch (start us, length us, event | category | flops | bytes accessed | tf_op | source)
XLA Modules:
  0.0 833.3 jit_solution(8870833214309930686)
XLA Ops:
  6.5 0.7 all-gather.5.cloned.1.call-update
  7.3 0.7 compare_select_fusion
  8.3 0.7 compare_and_fusion
  9.2 1.8 slice_bitcast_fusion
  11.0 42.7 %all-gather.5.cloned.1.call-done = bf16[8192,128]{1,0:T(8,128)(2,1)} async-done(((bf16[512,128]{1,0:T(8,128)(2,1)}), bf16[8192,128]{1,0:T(8,128)(2,1)}) %all-gather.5.cloned.1.call-update) | async-done | bytes 2097168 | tf_op jit(solution)/shard_map/all_gather | solution.py:48
  53.7 36.6 %gather_fusion = bf16[1536,128,128]{2,1,0:T(8,128)(2,1)} fusion(bf16[64,128,128]{2,1,0:T(8,128)(2,1)} %bitcast.97, s32[2048]{0:T(1024)S(1)} %pad_clamp_fusion), kind=kCustom, calls=%fused_computation.clone | custom fusion | bytes 100669440 | tf_op jit(solution)/shard_map/jit(_take)/gather | solution.py:26
  90.3 64.5 %copy.60 = bf16[1536,128,128]{1,2,0:T(8,128)(2,1)} copy(bf16[1536,128,128]{2,1,0:T(8,128)(2,1)} %gather_fusion) | data formatting | bytes 100663296 | tf_op jit(solution)/shard_map/jit(_take)/gather | solution.py:26
  154.9 40.1 %fusion.6 = f32[256,128,128,1]{2,1,3,0:T(8,128)} fusion(bf16[256,6,128,128]{3,2,1,0:T(8,128)(2,1)} %param.7, bf16[256,6,128,128]{2,3,1,0:T(8,128)(2,1)} %bitcast.104, pred[256,6]{1,0:T(8,128)(4,1)S(1)} %copy.55), kind=kOutput, calls=%fused_computation.10 | convolution fusion | flops 6467616768 | bytes 117442048 | tf_op jit(solution)/shard_map/pkab,pkbq->paq/dot_general | solution.py:27
  195.0 12.9 %bitcast_reduce_fusion.3 = (f32[4,128,128]{1,2,0:T(8,128)S(1)}, f32[256,128,128]{1,2,0:T(8,128)}) fusion(bf16[4,128,128]{2,1,0:T(8,128)(2,1)S(1)} %copy-done.3, s32[256,128]{1,0:T(8,128)S(1)} %get-tuple-element.8, f32[256,128,128,1]{2,1,3,0:T(8,128)} %fusion.6), kind=kOutput, calls=%fused_computation.37 | convolution fusion | flops 1086259200 | bytes 33980416 | tf_op jit(solution)/shard_map/pbr,rq->pbq/dot_general | solution.py:31
  207.9 8.0 fusion.23
  215.9 0.8 copy.62
  216.9 40.1 %all-gather.7.cloned.1.call-done = bf16[8192,128]{1,0:T(8,128)(2,1)} async-done(((bf16[512,128]{1,0:T(8,128)(2,1)}), bf16[8192,128]{1,0:T(8,128)(2,1)}) %all-gather.7.cloned.1.call-update) | async-done | bytes 2097168 | tf_op jit(solution)/shard_map/all_gather | solution.py:59
  257.0 36.6 %gather_fusion.1 = bf16[1536,128,128]{2,1,0:T(8,128)(2,1)} fusion(bf16[64,128,128]{2,1,0:T(8,128)(2,1)} %bitcast.98, s32[2048]{0:T(1024)S(1)} %pad_clamp_fusion), kind=kCustom, calls=%fused_computation.1.clone | custom fusion | bytes 100669440 | tf_op jit(solution)/shard_map/jit(_take)/gather | solution.py:26
  293.6 64.5 %copy.64 = bf16[256,6,128,128]{2,3,1,0:T(8,128)(2,1)} copy(bf16[256,6,128,128]{3,2,1,0:T(8,128)(2,1)} %bitcast.102) | data formatting | bytes 100663296 | tf_op jit(solution)/shard_map/jit(_take)/gather | solution.py:26
  358.2 40.1 %fusion.4 = f32[256,128,128,1]{2,1,3,0:T(8,128)} fusion(bf16[256,6,128,128]{3,2,1,0:T(8,128)(2,1)} %param.7, bf16[256,6,128,128]{2,3,1,0:T(8,128)(2,1)} %copy.64, pred[256,6]{1,0:T(8,128)(4,1)S(1)} %copy.55), kind=kOutput, calls=%fused_computation.8 | convolution fusion | flops 6467616768 | bytes 117442048 | tf_op jit(solution)/shard_map/pkab,pkbq->paq/dot_general | solution.py:27
  398.3 12.9 %bitcast_reduce_fusion.2 = (f32[4,128,128]{1,2,0:T(8,128)S(1)}, f32[256,128,128]{1,2,0:T(8,128)}) fusion(bf16[4,128,128]{2,1,0:T(8,128)(2,1)S(1)} %copy-done.3, s32[256,128]{1,0:T(8,128)S(1)} %copy-done.2, f32[256,128,128,1]{2,1,3,0:T(8,128)} %fusion.4), kind=kOutput, calls=%fused_computation.33 | convolution fusion | flops 1086259200 | bytes 33980416 | tf_op jit(solution)/shard_map/pbr,rq->pbq/dot_general | solution.py:31
  411.2 8.0 fusion.21
  419.2 0.8 copy.66
  420.3 40.0 %all-gather.9.cloned.1.call-done = bf16[8192,128]{1,0:T(8,128)(2,1)} async-done(((bf16[512,128]{1,0:T(8,128)(2,1)}), bf16[8192,128]{1,0:T(8,128)(2,1)}) %all-gather.9.cloned.1.call-update) | async-done | bytes 2097168 | tf_op jit(solution)/shard_map/all_gather | solution.py:59
  460.3 36.6 %gather_fusion.2 = bf16[1536,128,128]{2,1,0:T(8,128)(2,1)} fusion(bf16[64,128,128]{2,1,0:T(8,128)(2,1)} %bitcast.99, s32[2048]{0:T(1024)S(1)} %pad_clamp_fusion), kind=kCustom, calls=%fused_computation.2.clone | custom fusion | bytes 100669440 | tf_op jit(solution)/shard_map/jit(_take)/gather | solution.py:26
  496.9 64.5 %copy.68 = bf16[256,6,128,128]{2,3,1,0:T(8,128)(2,1)} copy(bf16[256,6,128,128]{3,2,1,0:T(8,128)(2,1)} %bitcast.103) | data formatting | bytes 100663296 | tf_op jit(solution)/shard_map/jit(_take)/gather | solution.py:26
  561.5 40.1 %fusion.2 = f32[256,128,128,1]{2,1,3,0:T(8,128)} fusion(bf16[256,6,128,128]{3,2,1,0:T(8,128)(2,1)} %param.7, bf16[256,6,128,128]{2,3,1,0:T(8,128)(2,1)} %copy.68, pred[256,6]{1,0:T(8,128)(4,1)S(1)} %copy.55), kind=kOutput, calls=%fused_computation.6 | convolution fusion | flops 6467616768 | bytes 117442048 | tf_op jit(solution)/shard_map/pkab,pkbq->paq/dot_general | solution.py:27
  601.6 12.9 %bitcast_reduce_fusion.1 = (f32[4,128,128]{1,2,0:T(8,128)S(1)}, f32[256,128,128]{1,2,0:T(8,128)}) fusion(bf16[4,128,128]{2,1,0:T(8,128)(2,1)S(1)} %copy-done.3, s32[256,128]{1,0:T(8,128)S(1)} %copy-done.1, f32[256,128,128,1]{2,1,3,0:T(8,128)} %fusion.2), kind=kOutput, calls=%fused_computation.29 | convolution fusion | flops 1086259200 | bytes 33980416 | tf_op jit(solution)/shard_map/pbr,rq->pbq/dot_general | solution.py:31
  614.5 8.0 fusion.19
  622.6 0.8 copy.70
  623.3 40.3 %all-gather.11.cloned.1.call-done = bf16[8192,128]{1,0:T(8,128)(2,1)} async-done(((bf16[512,128]{1,0:T(8,128)(2,1)}), bf16[8192,128]{1,0:T(8,128)(2,1)}) %all-gather.11.cloned.1.call-update) | async-done | bytes 2097168 | tf_op jit(solution)/shard_map/all_gather | solution.py:59
  663.6 36.6 %gather_fusion.3 = bf16[1536,128,128]{2,1,0:T(8,128)(2,1)} fusion(bf16[64,128,128]{2,1,0:T(8,128)(2,1)} %bitcast.100, s32[2048]{0:T(1024)S(1)} %pad_clamp_fusion), kind=kCustom, calls=%fused_computation.3.clone | custom fusion | bytes 100669440 | tf_op jit(solution)/shard_map/jit(_take)/gather | solution.py:26
  700.3 64.5 %copy.72 = bf16[256,6,128,128]{2,3,1,0:T(8,128)(2,1)} copy(bf16[256,6,128,128]{3,2,1,0:T(8,128)(2,1)} %bitcast.101) | data formatting | bytes 100663296 | tf_op jit(solution)/shard_map/jit(_take)/gather | solution.py:26
  764.8 40.2 %fusion = f32[256,128,128,1]{2,1,3,0:T(8,128)} fusion(bf16[256,6,128,128]{3,2,1,0:T(8,128)(2,1)} %param.7, bf16[256,6,128,128]{2,3,1,0:T(8,128)(2,1)} %copy.72, pred[256,6]{1,0:T(8,128)(4,1)S(1)} %copy.55), kind=kOutput, calls=%fused_computation.4 | convolution fusion | flops 6467616768 | bytes 117442048 | tf_op jit(solution)/shard_map/pkab,pkbq->paq/dot_general | solution.py:27
  805.0 12.9 %bitcast_reduce_fusion = (f32[4,128,128]{1,2,0:T(8,128)S(1)}, f32[256,128,128]{1,2,0:T(8,128)}) fusion(bf16[4,128,128]{2,1,0:T(8,128)(2,1)S(1)} %copy-done.3, s32[256,128]{1,0:T(8,128)S(1)} %copy-done, f32[256,128,128,1]{2,1,3,0:T(8,128)} %fusion), kind=kOutput, calls=%fused_computation.25 | convolution fusion | flops 1086259200 | bytes 33980416 | tf_op jit(solution)/shard_map/pbr,rq->pbq/dot_general | solution.py:31
  817.8 8.0 fusion.17
  825.9 0.8 copy.74
  (23 shorter events, 1.2 us)
Async XLA Ops:
  6.5 47.2 %all-gather.5.cloned.1.call-start = ((), (), s32[]{:S(2)}) async-start(), calls=%async_computation | async-start | bytes 2228224 | tf_op jit(solution)/shard_map/all_gather | solution.py:48
  7.3 249.8 %all-gather.7.cloned.1.call-start = ((), (), s32[]{:S(2)}) async-start(), calls=%async_computation.1 | async-start | bytes 2228224 | tf_op jit(solution)/shard_map/all_gather | solution.py:59
  154.9 40.1 %copy-start.3 = (bf16[4,128,128]{2,1,0:T(8,128)(2,1)S(1)}, bf16[4,128,128]{2,1,0:T(8,128)(2,1)}, u32[]{:S(2)}) copy-start(bf16[4,128,128]{2,1,0:T(8,128)(2,1)} %param.10) | copy-start | bytes 393220
  216.7 243.6 %all-gather.9.cloned.1.call-start = ((), (), s32[]{:S(2)}) async-start(), calls=%async_computation.2 | async-start | bytes 2228224 | tf_op jit(solution)/shard_map/all_gather | solution.py:59
  358.2 40.1 %copy-start.2 = (s32[256,128]{1,0:T(8,128)S(1)}, s32[256,128]{1,0:T(8,128)}, u32[]{:S(2)}) copy-start(s32[256,128]{1,0:T(8,128)} %get-tuple-element.7) | copy-start | bytes 393220
  420.0 243.6 %all-gather.11.cloned.1.call-start = ((), (), s32[]{:S(2)}) async-start(), calls=%async_computation.3 | async-start | bytes 2228224 | tf_op jit(solution)/shard_map/all_gather | solution.py:59
  561.5 40.1 %copy-start.1 = (s32[256,128]{1,0:T(8,128)S(1)}, s32[256,128]{1,0:T(8,128)}, u32[]{:S(2)}) copy-start(s32[256,128]{1,0:T(8,128)} %get-tuple-element.9) | copy-start | bytes 393220
  764.8 40.2 %copy-start = (s32[256,128]{1,0:T(8,128)S(1)}, s32[256,128]{1,0:T(8,128)}, u32[]{:S(2)}) copy-start(s32[256,128]{1,0:T(8,128)} %get-tuple-element.6) | copy-start | bytes 393220
Sparse Core Ops, SparseCore 0:
  9.5 44.1 all-gather.4
  216.8 40.1 all-gather.6
  420.1 40.1 all-gather.8
  623.5 40.1 all-gather.10
where the time goes:
time: 841 us; the launch traced here: 833 us
  local copies, waits for them, and re-layouts  410 us (49%)
  matrix products  212 us (25%)
  waiting for transfers between devices  164 us (20%)
  other arithmetic  33.7 us (4%)
  between operations  13.2 us (2%)
    gather x8, local copies, waits for them, and re-layouts, choice_partials(): picked = jnp.take(stacked, col_block, axis=0)  405 us
    dot_general x4, matrix products, choice_partials(): jnp.einsum('pkab,pkbq->paq', transitions, picked, preferred_element_type=...  160 us
    all_gather x3, waiting for transfers between devices, shards(): lax.all_gather(block_values.astype(jnp.bfloat16), 'choice', axis=0, tiled...  120 us
    dot_general x4, matrix products, choice_partials(): jnp.einsum('pbr,rq->pbq', onehot, reward_rows, preferred_element_type=jnp...  51.5 us
    all_gather x1, waiting for transfers between devices, shards(): next_values = lax.all_gather(terminal, 'choice', axis=0, tiled=True)  42.7 us
    reduce_sum x4, other arithmetic, choice_partials(): totals = jnp.sum(jnp.exp(grouped - highest[:, None]), axis=1)  32.1 us
  transfers between devices with their start and end apart: 4, of which 4 were waited for; matrix products, arithmetic and copies ran while one was open for 0% of the time, Pallas kernels for 0%

commit v1 on v0

--- a/solution.py
+++ b/solution.py
@@ -1,6 +1,10 @@
+import functools
+
 import jax
 import jax.numpy as jnp
 from jax import lax
+from jax.experimental import pallas as pl
+from jax.experimental.pallas import tpu as pltpu
 from jax.sharding import PartitionSpec as P
 
 J = 64
@@ -37,7 +41,7 @@
     return (highest.reshape(-1, columns), totals.reshape(-1, columns))
 
 
-def shards(transitions, col_block, reward_class, reward_table, terminal):
+def shards_split(transitions, col_block, reward_class, reward_table, terminal):
     devices = lax.axis_size("choice")
     pair_count = transitions.shape[0]
     inner_count = min(J, pair_count)
@@ -72,6 +76,235 @@
     return result
 
 
+CHUNK = 8
+MESH = pl.DeviceIdType.MESH
+
+
+def chunk_scores(first, cols_ref, trans_ref, classes, table, load_block, scores_ref):
+    size = trans_ref.shape[2]
+    types = table.shape[0]
+    depth = trans_ref.shape[1]
+    kinds = lax.broadcasted_iota(jnp.int32, (types, size), 0)
+    for i in range(CHUNK):
+        blocks = [load_block(cols_ref[(first + i) * depth + k]) for k in range(depth)]
+        left = jnp.concatenate([trans_ref[i, k] for k in range(depth)], axis=1)
+        right = jnp.concatenate(blocks, axis=0)
+        onehot = jnp.where(classes[i : i + 1, :] == kinds, 1.0, 0.0).astype(jnp.bfloat16)
+        scores_ref[i] = jnp.dot(
+            left, right, preferred_element_type=jnp.float32
+        ) + lax.dot_general(
+            onehot, table, (((0,), (0,)), ((), ())), preferred_element_type=jnp.float32
+        )
+
+
+def fold(scores_ref, high_ref, total_ref):
+    before = high_ref[...]
+    high = before
+    for i in range(CHUNK):
+        high = jnp.maximum(high, scores_ref[i])
+    total = total_ref[...] * jnp.exp(before - high)
+    for i in range(CHUNK):
+        total = total + jnp.exp(scores_ref[i] - high)
+    high_ref[...] = high
+    total_ref[...] = total
+
+
+def age_kernel(cols_ref, trans_ref, class_ref, table_ref, value_ref, out_ref, scores_ref, high_ref, total_ref):
+    row, step = pl.program_id(0), pl.program_id(1)
+    steps = pl.num_programs(1)
+
+    @pl.when(step == 0)
+    def _():
+        high_ref[...] = jnp.full_like(high_ref, -jnp.inf)
+        total_ref[...] = jnp.zeros_like(total_ref)
+
+    chunk_scores(
+        (row * steps + step) * CHUNK, cols_ref, trans_ref, class_ref[0], table_ref[0],
+        lambda c: value_ref[c], scores_ref,
+    )
+    fold(scores_ref, high_ref, total_ref)
+
+    @pl.when(step == steps - 1)
+    def _():
+        out_ref[0] = (high_ref[...] + jnp.log(total_ref[...])).astype(out_ref.dtype)
+
+
+def one_age(age, cols, transitions, reward_class, reward_table, values, kind):
+    pairs, depth, size, _ = transitions.shape
+    types, columns = reward_table.shape[1:]
+    rows, steps = pairs // J, J // CHUNK
+    return pl.pallas_call(
+        age_kernel,
+        out_shape=jax.ShapeDtypeStruct((rows, size, columns), kind),
+        grid_spec=pltpu.PrefetchScalarGridSpec(
+            num_scalar_prefetch=1,
+            grid=(rows, steps),
+            in_specs=[
+                pl.BlockSpec((CHUNK, depth, size, size), lambda r, s, c: (r * steps + s, 0, 0, 0)),
+                pl.BlockSpec((1, CHUNK, size), lambda r, s, c: (age, r * steps + s, 0)),
+                pl.BlockSpec((1, types, columns), lambda r, s, c: (age, 0, 0)),
+                pl.BlockSpec(memory_space=pltpu.VMEM),
+            ],
+            out_specs=pl.BlockSpec((1, size, columns), lambda r, s, c: (r, 0, 0)),
+            scratch_shapes=[
+                pltpu.VMEM((CHUNK, size, columns), jnp.float32),
+                pltpu.VMEM((size, columns), jnp.float32),
+                pltpu.VMEM((size, columns), jnp.float32),
+            ],
+        ),
+        cost_estimate=pl.CostEstimate(
+            flops=2 * pairs * (depth * size + types) * size * columns,
+            bytes_accessed=transitions.size * 2,
+            transcendentals=pairs * size * columns,
+        ),
+    )(cols, transitions, reward_class, reward_table, values)
+
+
+class Spread:
+    def __init__(self, values, send, recv):
+        self.values, self.send, self.recv = values, send, recv
+        devices = lax.axis_size("choice")
+        self.group = lax.axis_index("groups")
+        self.me = lax.axis_index("choice")
+        self.core, self.x, self.z = self.me % 2, (self.me // 2) % 2, self.me // 4
+        self.depth = devices // 4
+        self.across = self.place(self.z, 1 - self.x, self.core)
+        self.beside = self.place(self.z, self.x, 1 - self.core)
+        self.mates = [
+            self.place((self.z + d) % self.depth, self.x, self.core) for d in range(1, self.depth)
+        ]
+
+    def place(self, z, x, core):
+        return z * 4 + x * 2 + core
+
+    def copy(self, way, rows, b, origin, target, source=None):
+        block = self.values.at[origin * rows + b]
+        return pltpu.make_async_remote_copy(
+            src_ref=block if source is None else source,
+            dst_ref=block,
+            send_sem=self.send.at[b, way],
+            recv_sem=self.recv.at[b, origin],
+            device_id=(self.group, target),
+            device_id_type=MESH,
+        )
+
+    def greet(self):
+        barrier = pltpu.get_barrier_semaphore()
+        near = self.mates + [self.across, self.beside]
+        for target in near:
+            pl.semaphore_signal(barrier, inc=1, device_id=(self.group, target), device_id_type=MESH)
+        pl.semaphore_wait(barrier, len(near))
+
+    def own(self, rows, b, source=None):
+        d = self.depth
+        out = [self.copy(i, rows, b, self.me, t, source) for i, t in enumerate(self.mates)]
+        out.append(self.copy(d - 1, rows, b, self.me, self.across, source))
+        out.append(self.copy(d, rows, b, self.me, self.beside, source))
+        return out
+
+    def along(self, rows, b):
+        d = self.depth
+        out = []
+        for i, origin in enumerate(self.mates):
+            out.append(self.copy(d + 1 + 2 * i, rows, b, origin, self.across))
+            out.append(self.copy(d + 2 + 2 * i, rows, b, origin, self.beside))
+        return out
+
+    def over(self, rows, b):
+        d = self.depth
+        return [
+            self.copy(3 * d - 1 + i, rows, b, self.place((self.z + i) % d, 1 - self.x, self.core), self.beside)
+            for i in range(d)
+        ]
+
+    def last(self, rows, b):
+        return [
+            self.copy(0, rows, b, self.place((self.z + i) % self.depth, x, 1 - self.core), self.beside)
+            for i in range(self.depth)
+            for x in (0, 1)
+        ]
+
+    def start_own(self, rows, b, source=None):
+        for c in self.own(rows, b, source):
+            c.start()
+
+    def start_along(self, rows, b):
+        out = self.along(rows, b)
+        for i in range(len(self.mates)):
+            out[2 * i].wait_recv()
+            out[2 * i].start()
+            out[2 * i + 1].start()
+
+    def start_over(self, rows, b):
+        for c in self.over(rows, b):
+            c.wait_recv()
+            c.start()
+
+    def finish(self, rows, b):
+        for c in self.last(rows, b):
+            c.wait_recv()
+
+    def drain(self, rows, b):
+        for c in self.own(rows, b) + self.along(rows, b) + self.over(rows, b):
+            c.wait_send()
+
+
+def ways(devices):
+    return 4 * (devices // 4) - 1
+
+
+def gather_kernel(own_ref, out_ref, send, recv, local):
+    rows = own_ref.shape[0]
+    spread = Spread(out_ref, send, recv)
+    keep = pltpu.make_async_copy(own_ref, out_ref.at[pl.ds(spread.me * rows, rows)], local)
+    keep.start()
+    spread.greet()
+    for b in range(rows):
+        spread.start_own(rows, b, own_ref.at[b])
+    for b in range(rows):
+        spread.start_along(rows, b)
+    for b in range(rows):
+        spread.start_over(rows, b)
+    for b in range(rows):
+        spread.finish(rows, b)
+    for b in range(rows):
+        spread.drain(rows, b)
+    keep.wait()
+
+
+def gather(own):
+    devices = lax.axis_size("choice")
+    rows, size, columns = own.shape
+    return pl.pallas_call(
+        gather_kernel,
+        out_shape=jax.ShapeDtypeStruct((rows * devices, size, columns), own.dtype),
+        in_specs=[pl.BlockSpec(memory_space=pltpu.VMEM)],
+        out_specs=pl.BlockSpec(memory_space=pltpu.VMEM),
+        scratch_shapes=[
+            pltpu.SemaphoreType.DMA((rows, ways(devices))),
+            pltpu.SemaphoreType.DMA((rows, devices)),
+            pltpu.SemaphoreType.DMA,
+        ],
+        compiler_params=pltpu.CompilerParams(collective_id=0, has_side_effects=True),
+    )(own)
+
+
+def shards_whole(transitions, col_block, reward_class, reward_table, terminal):
+    size = transitions.shape[2]
+    cols = col_block.reshape(-1)
+    values = terminal.reshape(terminal.shape[0] // size, size, terminal.shape[1])
+    for age in range(AGES - 1, -1, -1):
+        kind = jnp.bfloat16 if age > 0 else jnp.float32
+        values = one_age(age, cols, transitions, reward_class, reward_table, gather(values), kind)
+    return values.reshape(terminal.shape)
+
+
+def shards(transitions, col_block, reward_class, reward_table, terminal):
+    whole = transitions.shape[0] % J == 0 and lax.axis_size("choice") % 4 == 0
+    body = shards_whole if whole else shards_split
+    return body(transitions, col_block, reward_class, reward_table, terminal)
+
+
 def solution(mesh):
     return jax.shard_map(
         shards,

time: 841 us -> 257 us (0.31)
  local copies, waits for them, and re-layouts: 410 us -> 1.56 us
  Pallas kernels: 0 us -> 253 us
  matrix products: 212 us -> 0 us
  waiting for transfers between devices: 164 us -> 0 us
  other arithmetic: 33.7 us -> 0 us
  between operations: 13.2 us -> 0.04 us
    gather x8 -> x0, local copies, waits for them, and re-layouts: 405 us -> none  [choice_partials(): picked = jnp.take(stacked, col_block, axis=0)]
    pallas_call x0 -> x8, Pallas kernels: none -> 253 us  [the longest x4 157 us: one_age(): pl.pallas_call(age_kernel, out_shape=jax.ShapeDtypeStruct((rows, size, co...]
    dot_general x8 -> x0, matrix products: 212 us -> none  [the longest x4 160 us: choice_partials(): jnp.einsum('pkab,pkbq->paq', transitions, picked, preferred_element_type=...]
    all_gather x4 -> x0, waiting for transfers between devices: 163 us -> none  [the longest x3 120 us: shards(): lax.all_gather(block_values.astype(jnp.bfloat16), 'choice', axis=0, tiled...]
    reduce_sum x4 -> x0, other arithmetic: 32.1 us -> none  [choice_partials(): totals = jnp.sum(jnp.exp(grouped - highest[:, None]), axis=1)]
  transfers between devices with their start and end apart: 4 -> 0, of which waited for: 4 -> 0; matrix products, arithmetic and copies ran while one was open for 0% -> 0% of each run, Pallas kernels for 0% -> 0%
where the time goes in v1:
time: 257 us; the launch traced here: 255 us
  Pallas kernels  253 us (98%)
    pallas_call x4, Pallas kernels, one_age(): pl.pallas_call(age_kernel, out_shape=jax.ShapeDtypeStruct((rows, size, co...  157 us
    pallas_call x4, Pallas kernels, gather(): pl.pallas_call(gather_kernel, out_shape=jax.ShapeDtypeStruct((rows * devi...  95.9 us

profile of v1, /device:TPU:0, one launch (start us, length us, event | category | flops | bytes accessed | tf_op | source)
XLA Modules:
  0.0 254.8 jit_solution(9903482274036019259)
XLA Ops:
  0.0 0.8 copy.6
  0.8 0.7 reshape.9.cols_ref
  1.6 25.6 %shard_map.55.value_ref = bf16[64,128,128]{2,1,0:T(8,128)(2,1)} custom-call(bf16[4,128,128]{2,1,0:T(8,128)(2,1)} %bitcast.2), custom_call_target="tpu_custom_call" | custom-call | tf_op jit(solution)/shard_map/pallas_call | solution.py:278
  27.2 39.3 %shard_map.56.own_ref = bf16[4,128,128]{2,1,0:T(8,128)(2,1)} custom-call(s32[1536]{0:T(1024)} %reshape.9.cols_ref, bf16[256,6,128,128]{3,2,1,0:T(8,128)(2,1)} %trans_ref.7, s32[4,256,128]{2,1,0:T(8,128)} %class_ref.7, bf16[4,128,128]{2,1,0:T(8,128)(2,1)} %table_ref.7, bf16[64,128,128]{2,1,0:T(8,128)(2,1)} %shard_map.55.value_ref), custom_call_target="tpu_custom_call" | custom-call | flops 7516192768 | bytes 50331648 | tf_op jit(solution)/shard_map/pallas_call | solution.py:136
  66.5 22.6 %shard_map.57.value_ref = bf16[64,128,128]{2,1,0:T(8,128)(2,1)} custom-call(bf16[4,128,128]{2,1,0:T(8,128)(2,1)} %shard_map.56.own_ref), custom_call_target="tpu_custom_call" | custom-call | tf_op jit(solution)/shard_map/pallas_call | solution.py:278
  89.1 39.3 %shard_map.58.own_ref = bf16[4,128,128]{2,1,0:T(8,128)(2,1)} custom-call(s32[1536]{0:T(1024)} %reshape.9.cols_ref, bf16[256,6,128,128]{3,2,1,0:T(8,128)(2,1)} %trans_ref.7, s32[4,256,128]{2,1,0:T(8,128)} %class_ref.7, bf16[4,128,128]{2,1,0:T(8,128)(2,1)} %table_ref.7, bf16[64,128,128]{2,1,0:T(8,128)(2,1)} %shard_map.57.value_ref), custom_call_target="tpu_custom_call" | custom-call | flops 7516192768 | bytes 50331648 | tf_op jit(solution)/shard_map/pallas_call | solution.py:136
  128.4 24.3 %shard_map.59.value_ref = bf16[64,128,128]{2,1,0:T(8,128)(2,1)} custom-call(bf16[4,128,128]{2,1,0:T(8,128)(2,1)} %shard_map.58.own_ref), custom_call_target="tpu_custom_call" | custom-call | tf_op jit(solution)/shard_map/pallas_call | solution.py:278
  152.6 39.3 %shard_map.60.own_ref = bf16[4,128,128]{2,1,0:T(8,128)(2,1)} custom-call(s32[1536]{0:T(1024)} %reshape.9.cols_ref, bf16[256,6,128,128]{3,2,1,0:T(8,128)(2,1)} %trans_ref.7, s32[4,256,128]{2,1,0:T(8,128)} %class_ref.7, bf16[4,128,128]{2,1,0:T(8,128)(2,1)} %table_ref.7, bf16[64,128,128]{2,1,0:T(8,128)(2,1)} %shard_map.59.value_ref), custom_call_target="tpu_custom_call" | custom-call | flops 7516192768 | bytes 50331648 | tf_op jit(solution)/shard_map/pallas_call | solution.py:136
  191.9 23.5 %shard_map.61.value_ref = bf16[64,128,128]{2,1,0:T(8,128)(2,1)} custom-call(bf16[4,128,128]{2,1,0:T(8,128)(2,1)} %shard_map.60.own_ref), custom_call_target="tpu_custom_call" | custom-call | tf_op jit(solution)/shard_map/pallas_call | solution.py:278
  215.4 39.3 %shard_map.62 = f32[4,128,128]{2,1,0:T(8,128)} custom-call(s32[1536]{0:T(1024)} %reshape.9.cols_ref, bf16[256,6,128,128]{3,2,1,0:T(8,128)(2,1)} %trans_ref.7, s32[4,256,128]{2,1,0:T(8,128)} %class_ref.7, bf16[4,128,128]{2,1,0:T(8,128)(2,1)} %table_ref.7, bf16[64,128,128]{2,1,0:T(8,128)(2,1)} %shard_map.61.value_ref), custom_call_target="tpu_custom_call" | custom-call | flops 7516192768 | bytes 50331648 | tf_op jit(solution)/shard_map/pallas_call | solution.py:136
